TPU v7x, 32 devices: a whole 2x2x4 slice. The times are simulated.
32 devices in a mesh: group: 2 (over x), seq: 16 (over z, y, core).
Axes of the slice: x: 2, y: 2, z: 4, core: 2. Of those that a mesh axis runs over, the one named last changes fastest.
Arguments:
- resid_in: bfloat16 [512, 2880], P(('group', 'seq')), parts along dimension 0, may hold values from -6 to 6
- queries: bfloat16 [512, 4096], P('group'), parts along dimension 0, may hold values from -256 to 256
- key_cache: bfloat16 [8, 8192, 512], P('group', 'seq'), parts along dimension 0, may hold values from -6 to 6
- value_cache: bfloat16 [8, 8192, 512], P('group', 'seq'), parts along dimension 0, may hold values from -6 to 6
- lengths: int32 [8], P('group'), parts along dimension 0, may hold values from 8 to 8128, as said below
- expert_ids: int32 [512, 4], P(('group', 'seq')), parts along dimension 0, may hold values from 0 to 15, all different within a row; in each aligned block of 16 rows (0 to 15, 16 to 31, ...) at most 8 rows name the same one
- expert_weights: float32 [512, 4], P(('group', 'seq')), parts along dimension 0, may hold values from 0.1 to 0.6
- out_proj: bfloat16 [4096, 2880], P('seq'), may hold values from -0.09375 to 0.09375
- gate_proj: bfloat16 [2880, 23040], P(None, 'seq'), may hold values from -0.109375 to 0.109375
- up_proj: bfloat16 [2880, 23040], P(None, 'seq'), may hold values from -0.109375 to 0.109375
- down_proj: bfloat16 [23040, 2880], P('seq'), may hold values from -0.15625 to 0.15625
- moe_gain: float32 [2880], replicated, may hold values from 0.5 to 2
- attn_gain: float32 [2880], replicated, may hold values from 0.5 to 2
- query_proj: bfloat16 [2880, 4096], P(None, 'seq'), may hold values from -0.109375 to 0.109375
Outputs:
- stream_out: bfloat16 [512, 2880], P(('group', 'seq')), parts along dimension 0
- next_queries: bfloat16 [512, 4096], P('group', 'seq'), parts along dimension 0
There are 2 independent parts, one for each index of `group`. A program takes and returns all parts, laid end to end along the dimension named above; an argument that names none is the same for every part. Nothing has to cross between parts.
Inputs may be any that keep to these rules, and one draw needn't show every extreme that they name: `expert_ids`: in each aligned block of 16 rows (the rows of one device) no expert is named by more than 8 rows, a bound that some block reaches. `lengths`: some request has exactly 8128 cached positions.
All inputs are finite; a program needn't handle non-finite values.
Results may differ from a plain program's by a relative error of at most 0.012.
Values may be sent and summed in bfloat16 or wider, within the bound.
A program may use at most 128 MiB of HBM per device.

v0:
```python
import functools
import jax
import jax.numpy as jnp
from jax import lax
from jax.experimental import pallas as pl
from jax.experimental.pallas import tpu as pltpu
from jax.sharding import PartitionSpec as P

H = 64
KVH = 8
HEAD_SIZE = 64
EXPERTS = 16
QROWS = 64
NEG_FILL = -1e30
PIECES = 4
MESH = pl.DeviceIdType.MESH
STEPS = KVH // 2


def place(i, order):
    out = 0
    for k in order:
        out = out * 2 + (i // 2**k) % 2
    return out


def chunks(total, size, body):
    full = total // size
    if full:

        def step(c, carry):
            body(pl.multiple_of(c * size, size), size)
            return carry

        lax.fori_loop(0, full, step, 0)
    if total % size:
        body(full * size, total % size)


def norm_of(values, gain):
    wide = values.astype(jnp.float32)
    scaled = wide * lax.rsqrt(jnp.mean(wide * wide, axis=-1, keepdims=True) + 1e-05)
    return (scaled * gain).astype(jnp.bfloat16)


def layer_kernel(
    n, orders, cuts, splits,
    len_ref, q_hbm, k_hbm, v_hbm, resid_ref, ids_ref, weights_ref, wo_hbm, gate_hbm, up_hbm,
    down_hbm, wq_hbm, g1_ref, g2_ref,
    stream_ref, nq_ref,
    qb, kb, vb, wo, gate, up, down, wq, accs, mts, acc_ins, mt_ins, parts, part_ins, parts2,
    part2_ins, rows1, rows2, joined, act, att, load_sems, send_sems, recv_sems,
):
    bits = n.bit_length() - 1
    me = lax.axis_index("seq")
    bit = [(me // 2**k) % 2 for k in range(bits)]
    partner = [me + (1 - 2 * bit[k]) * 2**k for k in range(bits)]
    tok, d = resid_ref.shape
    pieces = len(cuts)
    ends = cuts[1:] + (d,)
    per_shard = H // n
    per_piece = per_shard // splits
    requests, span = kb.shape[0], kb.shape[1]
    share = requests // 2
    lanes = share * QROWS
    slots = n // STEPS

    loads = {}

    def load(name, src, dst):
        copy = pltpu.make_async_copy(src, dst, load_sems.at[len(loads)])
        copy.start()
        loads[name] = copy

    for c in range(2):
        rows_c, reqs_c = pl.ds(c * lanes, lanes), pl.ds(c * share, share)
        load(("q", c), q_hbm.at[rows_c], qb.at[rows_c])
        load(("k", c), k_hbm.at[reqs_c], kb.at[reqs_c])
        load(("v", c), v_hbm.at[reqs_c], vb.at[reqs_c])
    load("wo", wo_hbm, wo)
    load("gate", gate_hbm, gate)
    load("up", up_hbm, up)
    load("down", down_hbm, down)
    load("wq", wq_hbm, wq)

    barrier = pltpu.get_barrier_semaphore()
    for k in range(bits):
        pl.semaphore_signal(barrier, inc=1, device_id={"seq": partner[k]}, device_id_type=MESH)

    pairs = H // KVH // 2
    width = pairs * QROWS
    low = lax.broadcasted_iota(jnp.int32, (span, 2 * HEAD_SIZE), 1) < HEAD_SIZE
    reach = (
        me * span
        + lax.broadcasted_iota(jnp.int32, (span, width), 0)
        - lax.broadcasted_iota(jnp.int32, (span, width), 1) % QROWS
    )

    def attend(g, c):
        at_g = [place(g * slots, order) for order in orders]
        for r in range(share):
            req = c * share + r
            allowed = reach <= len_ref[req]
            kv_lanes = pl.ds(pl.multiple_of(g * 128, 128), 128)
            kp = kb[req, :, kv_lanes]
            vp = vb[req, :, kv_lanes]
            kr = jnp.concatenate([kp[:, HEAD_SIZE:], kp[:, :HEAD_SIZE]], axis=1)
            zero = jnp.zeros_like(kp)
            for hh in range(2):
                ke = jnp.where(low, kr if hh else kp, zero)
                ko = jnp.where(low, zero, kp if hh else kr)
                first = g * 2 * pairs + hh * pairs
                qs = jnp.concatenate(
                    [
                        qb[
                            req * QROWS : (req + 1) * QROWS,
                            pl.ds(pl.multiple_of((first + j) * 128, 128), 128),
                        ]
                        for j in range(pairs)
                    ],
                    axis=0,
                ) * jnp.bfloat16(HEAD_SIZE**-0.5)
                vh = vp[:, hh * HEAD_SIZE : (hh + 1) * HEAD_SIZE]
                for p, kk in enumerate((ke, ko)):
                    s = lax.dot_general(
                        kk, qs, (((1,), (1,)), ((), ())), preferred_element_type=jnp.float32
                    )
                    s = jnp.where(allowed, s, NEG_FILL)
                    m = jnp.max(s, axis=0, keepdims=True)
                    ch = jnp.exp(s - jnp.maximum(m, NEG_FILL * 0.1))
                    t = jnp.sum(ch, axis=0, keepdims=True)
                    acc = lax.dot_general(
                        vh,
                        ch.astype(jnp.bfloat16),
                        (((0,), (0,)), ((), ())),
                        preferred_element_type=jnp.float32,
                    ).astype(jnp.bfloat16)
                    for j in range(pairs):
                        head = hh * (H // KVH) + 2 * j + p
                        part, w = divmod(head % per_shard, per_piece)
                        part = c * splits + part
                        slot = at_g[part % 2] + place(head // per_shard, orders[part % 2])
                        src = slice(j * QROWS, (j + 1) * QROWS)
                        dst = slice(r * QROWS, (r + 1) * QROWS)
                        accs[part][slot, w * HEAD_SIZE : (w + 1) * HEAD_SIZE, dst] = acc[:, src]
                        mts[part][slot, w, 0:1, dst] = m[:, src]
                        mts[part][slot, w, 1:2, dst] = t[:, src]

    def load_wait(*names):
        for name in names:
            loads[name].wait()

    sends = []

    def remote(src, dst, phase, j, k):
        copy = pltpu.make_async_remote_copy(
            src_ref=src,
            dst_ref=dst,
            send_sem=send_sems.at[phase, j],
            recv_sem=recv_sems.at[phase, j],
            device_id={"seq": partner[k]},
            device_id_type=MESH,
        )
        copy.start()
        sends.append(copy)
        return copy

    def land(j):
        return n - 2 * (n >> (j + 1))

    class Halving:
        def __init__(self, c, bufs, inboxes, phases, merge):
            self.order, self.bufs, self.inboxes = orders[c % 2], bufs, inboxes
            self.phases, self.merge, self.flying = phases, merge, {}
            self.keep, self.away, base = [], [], 0
            for j, k in enumerate(self.order):
                half = n >> (j + 1)
                self.away.append(base + (1 - bit[k]) * half)
                base = base + bit[k] * half
                self.keep.append(base)

        def start(self, j):
            half = n >> (j + 1)
            self.flying[j] = [
                remote(
                    buf.at[pl.ds(self.away[j], half)],
                    inbox.at[pl.ds(land(j), half)],
                    phase,
                    j,
                    self.order[j],
                )
                for buf, inbox, phase in zip(self.bufs, self.inboxes, self.phases)
            ]

        def finish(self, j):
            for copy in self.flying[j]:
                copy.wait_recv()
            if j < bits - 1:

                def step(x, carry):
                    self.merge(self.keep[j] + x, land(j) + x, False)
                    return carry

                lax.fori_loop(0, n >> (j + 1), step, 0)
                self.start(j + 1)
            else:
                self.merge(self.keep[j], land(j), True)

    def merge_heads(c):
        def merge(mine, other, last):
            acc, acc_in, mt, mt_in = accs[c], acc_ins[c], mts[c], mt_ins[c]
            for w in range(per_piece):
                m1, t1 = mt[mine, w, 0:1, :], mt[mine, w, 1:2, :]
                m2, t2 = mt_in[other, w, 0:1, :], mt_in[other, w, 1:2, :]
                m = jnp.maximum(m1, m2)
                f1 = jnp.exp(m1 - m)
                f2 = jnp.exp(m2 - m)
                t = t1 * f1 + t2 * f2
                rows_w = slice(w * HEAD_SIZE, (w + 1) * HEAD_SIZE)
                a = (
                    acc[mine, rows_w, :].astype(jnp.float32) * f1
                    + acc_in[other, rows_w, :].astype(jnp.float32) * f2
                )
                if last:
                    top = (c % splits * per_piece + w) * HEAD_SIZE
                    col = c // splits * lanes
                    att[top : top + HEAD_SIZE, col : col + lanes] = (a / t).astype(jnp.bfloat16)
                else:
                    mt[mine, w, 0:1, :] = m
                    mt[mine, w, 1:2, :] = t
                    acc[mine, rows_w, :] = a.astype(jnp.bfloat16)

        return merge

    def scatter_of(bufs, inboxes, phase):
        sums = {}

        def adder(c):
            def merge(mine, other, last):
                total = bufs[c][mine].astype(jnp.float32) + inboxes[c][other].astype(jnp.float32)
                if last:
                    sums[c] = total
                else:
                    bufs[c][mine] = total.astype(jnp.bfloat16)

            return merge

        return [Halving(c, [bufs[c]], [inboxes[c]], [phase + c], adder(c)) for c in range(pieces)], sums

    def gather(bufs, phase):
        bases = [place(me, orders[c % 2]) for c in range(pieces)]

        def start(c, j):
            region = bufs[c].at[pl.ds(bases[c], n >> (j + 1))]
            bases[c] = bases[c] - bit[orders[c % 2][j]] * (n >> (j + 1))
            return remote(region, region, phase + c, j, orders[c % 2][j])

        flying = [start(c, bits - 1) for c in range(pieces)]
        for j in reversed(range(bits)):
            for c in range(pieces):
                flying[c].wait_recv()
                if j:
                    flying[c] = start(c, j - 1)

    def join(bufs):
        for i in range(n):
            for c in range(pieces):
                joined[i * tok : (i + 1) * tok, cuts[c] : cuts[c] + bufs[c].shape[2]] = bufs[c][
                    place(i, orders[c % 2])
                ]

    def spread(bufs, c, start, size, val):
        for i in range(n):
            bufs[c][place(i, orders[c % 2]), :, pl.ds(start, size)] = val[i * tok : (i + 1) * tok]

    heads_sum = [
        Halving(c, [mts[c], accs[c]], [mt_ins[c], acc_ins[c]], [2 * splits + c, c], merge_heads(c))
        for c in range(2 * splits)
    ]
    load_wait(("q", 0), ("k", 0), ("v", 0))

    def first_half(g, carry):
        attend(g, 0)
        return carry

    lax.fori_loop(0, STEPS, first_half, 0)
    pl.semaphore_wait(barrier, bits)
    early, late = heads_sum[:splits], heads_sum[splits:]
    for one in early:
        one.start(0)
    load_wait(("q", 1), ("k", 1), ("v", 1))
    for g in range(STEPS):
        attend(g, 1)
        for one in early:
            one.finish(g)
    for one in late:
        one.start(0)
    for j in range(bits):
        for one in (early if j >= STEPS else []) + late:
            one.finish(j)

    load_wait("wo")
    attended = att[...].T
    exchange, sums = scatter_of(parts, part_ins, 4 * splits)
    for c in range(pieces):

        def project(start, size, c=c):
            val = lax.dot_general(
                attended,
                wo[pl.ds(cuts[c] + start, size), :],
                (((1,), (1,)), ((), ())),
                preferred_element_type=jnp.float32,
            ).astype(jnp.bfloat16)
            spread(parts, c, start, size, val)

        chunks(parts[c].shape[2], 256, project)
        exchange[c].start(0)
    for j in range(bits):
        for c in range(pieces):
            exchange[c].finish(j)
    hidden = (
        resid_ref[...].astype(jnp.float32) + jnp.concatenate([sums[c] for c in range(pieces)], axis=1)
    ).astype(jnp.bfloat16)
    normed_here = norm_of(hidden, g1_ref[...].reshape(1, d))
    expert_row = lax.broadcasted_iota(jnp.int32, (EXPERTS, tok), 0)
    picked = jnp.zeros((EXPERTS, tok), jnp.float32)
    for k in range(ids_ref.shape[0]):
        picked += jnp.where(ids_ref[k : k + 1, :] == expert_row, weights_ref[k : k + 1, :], 0.0)
    picked = picked.T
    upper = picked.astype(jnp.bfloat16)
    lower = (picked - upper.astype(jnp.float32)).astype(jnp.bfloat16)
    here = [place(me, orders[c % 2]) for c in range(pieces)]
    final = pieces - 1
    rest = d - cuts[final]
    for c in range(pieces):
        rows1[c][here[c], :, : ends[c] - cuts[c]] = normed_here[:, cuts[c] : ends[c]]
    spot = here[final]
    rows1[final][spot, :, rest:] = jnp.zeros((tok, rows1[final].shape[2] - rest), jnp.bfloat16)
    rows1[final][spot, :, rest : rest + EXPERTS] = upper
    rows1[final][spot, :, rest + EXPERTS : rest + 2 * EXPERTS] = lower
    gather(rows1, 4 * splits + pieces)

    load_wait("gate", "up", "down")
    join(rows1)
    normed = joined[:, :d]
    tags = joined[:, d:].astype(jnp.float32)
    expert = me // (n // EXPERTS)
    lane = lax.broadcasted_iota(jnp.int32, tags.shape, 1)
    weight = jnp.sum(
        jnp.where((lane == expert) | (lane == expert + EXPERTS), tags, 0.0), axis=1, keepdims=True
    )

    def inner(start, size):
        g = lax.dot_general(
            normed,
            gate[pl.ds(start, size), :],
            (((1,), (1,)), ((), ())),
            preferred_element_type=jnp.float32,
        )
        u = lax.dot_general(
            normed,
            up[pl.ds(start, size), :],
            (((1,), (1,)), ((), ())),
            preferred_element_type=jnp.float32,
        )
        act[:, pl.ds(start, size)] = ((u + 1.0) * g * jax.nn.sigmoid(1.702 * g)).astype(
            jnp.bfloat16
        )

    chunks(gate.shape[0], 256, inner)
    active = act[...]
    exchange, sums = scatter_of(parts2, part2_ins, 4 * splits + 2 * pieces)
    for c in range(pieces):

        def outer(start, size, c=c):
            val = (
                jnp.dot(
                    active,
                    down[:, pl.ds(cuts[c] + start, size)],
                    preferred_element_type=jnp.float32,
                )
                * weight
            ).astype(jnp.bfloat16)
            spread(parts2, c, start, size, val)

        chunks(parts2[c].shape[2], 256, outer)
        exchange[c].start(0)
    for j in range(bits):
        for c in range(pieces):
            exchange[c].finish(j)
    stream = (
        hidden.astype(jnp.float32) + jnp.concatenate([sums[c] for c in range(pieces)], axis=1)
    ).astype(jnp.bfloat16)
    stream_ref[...] = stream
    normed_next = norm_of(stream, g2_ref[...].reshape(1, d))
    for c in range(pieces):
        rows2[c][here[c]] = normed_next[:, cuts[c] : ends[c]]
    gather(rows2, 4 * splits + 3 * pieces)
    load_wait("wq")
    join(rows2)
    nq_ref[...] = jnp.dot(
        joined[:, :d], wq[...], preferred_element_type=jnp.float32
    ).astype(jnp.bfloat16)
    for copy in sends:
        copy.wait_send()


def local(
    resid_in,
    queries,
    key_cache,
    value_cache,
    lengths,
    expert_ids,
    expert_weights,
    out_proj,
    gate_proj,
    up_proj,
    down_proj,
    moe_gain,
    attn_gain,
    query_proj,
):
    n = lax.axis_size("seq")
    rows = queries.shape[0]
    tok, d = resid_in.shape
    per_shard = H // n
    bits = n.bit_length() - 1
    order = list(range(bits))
    orders = (tuple(order), tuple([0, 2, 1] + order[3:]))
    full = -(-(d + 2 * EXPERTS) // 128) * 128
    wide = -(-d // (PIECES * 256)) * 256
    cuts = tuple(range(0, d, wide))
    splits = 2 if per_shard % 2 == 0 else 1
    phases = 4 * splits + 4 * len(cuts)
    any_spec = pl.BlockSpec(memory_space=pl.ANY)
    vmem = pl.BlockSpec(memory_space=pltpu.VMEM)
    smem = pl.BlockSpec(memory_space=pltpu.SMEM)
    bf = jnp.bfloat16
    heads = per_shard * HEAD_SIZE
    widths = [b - a for a, b in zip(cuts, cuts[1:] + (d,))]
    tagged = widths[:-1] + [full - cuts[-1]]
    buf = lambda *shape: pltpu.VMEM(shape, bf)
    cols = lambda: tuple(buf(n, tok, w) for w in widths)
    acc = lambda: tuple(buf(n, heads // splits, rows // 2) for _ in range(2 * splits))
    mt_shape = (n, per_shard // splits, 2, rows // 2)
    mt = lambda: tuple(pltpu.VMEM(mt_shape, jnp.float32) for _ in range(2 * splits))
    return pl.pallas_call(
        functools.partial(layer_kernel, n, orders, cuts, splits),
        out_shape=(
            jax.ShapeDtypeStruct((tok, d), bf),
            jax.ShapeDtypeStruct((rows, query_proj.shape[1]), bf),
        ),
        in_specs=[smem] + [any_spec] * 3 + [vmem] * 3 + [any_spec] * 5 + [vmem, vmem],
        out_specs=(vmem, vmem),
        scratch_shapes=[
            buf(*queries.shape),
            buf(*key_cache.shape),
            buf(*value_cache.shape),
            buf(*out_proj.shape[::-1]),
            buf(*gate_proj.shape[::-1]),
            buf(*up_proj.shape[::-1]),
            buf(*down_proj.shape),
            buf(*query_proj.shape),
            acc(),
            mt(),
            acc(),
            mt(),
            cols(),
            cols(),
            cols(),
            cols(),
            tuple(buf(n, tok, w) for w in tagged),
            cols(),
            buf(rows, full),
            buf(rows, gate_proj.shape[1]),
            buf(heads, rows),
            pltpu.SemaphoreType.DMA((11,)),
            pltpu.SemaphoreType.DMA((phases, bits)),
            pltpu.SemaphoreType.DMA((phases, bits)),
        ],
        compiler_params=pltpu.CompilerParams(
            collective_id=0, has_side_effects=True, vmem_limit_bytes=62 * 2**20
        ),
    )(
        lengths, queries, key_cache, value_cache, resid_in, expert_ids.T, expert_weights.T,
        out_proj.T, gate_proj.T, up_proj.T, down_proj, query_proj, moe_gain, attn_gain,
    )


def solution(mesh):
    placed = (
        P(("group", "seq"), None),
        P("group", None),
        P("group", "seq", None),
        P("group", "seq", None),
        P("group"),
        P(("group", "seq"), None),
        P(("group", "seq"), None),
        P("seq", None),
        P(None, "seq"),
        P(None, "seq"),
        P("seq", None),
        P(),
        P(),
        P(None, "seq"),
    )
    return jax.shard_map(
        local,
        mesh=mesh,
        in_specs=placed,
        out_specs=(P(("group", "seq"), None), P("group", "seq")),
        check_vma=False,
    )
```

profile of v0, /device:TPU:1, one launch (start us, length us, event | category | flops | bytes accessed | tf_op | source)
XLA Modules:
  0.0 126.1 jit_solution(16731615026915484996)
XLA Ops:
  0.6 122.3 %shard_map.149 = (bf16[16,2880]{1,0:T(8,128)(2,1)}, bf16[256,256]{1,0:T(8,128)(2,1)}) custom-call(s32[4]{0:T(128)} %len_ref.1, bf16[256,4096]{1,0:T(8,128)(2,1)} %q_hbm.1, bf16[4,512,512]{2,1,0:T(8,128)(2,1)} %k_hbm.1, bf16[4,512,512]{2,1,0:T(8,128)(2,1)} %v_hbm.1, bf16[16,2880]{1,0:T(8,128)(2,1)} %resid_ref.1, s32[4,16]{1,0:T(4,128)} %bitcast.8, ...), custom_call_target="tpu_custom_call" | custom-call | tf_op jit(solution)/shard_map/pallas_call | solution.py:448
  123.0 1.5 %copy.18 = bf16[16,2880]{1,0:T(8,128)(2,1)} copy(bf16[16,2880]{1,0:T(8,128)(2,1)} %get-tuple-element.4) | data formatting | bytes 184320
  124.5 1.6 %copy.19 = bf16[256,256]{1,0:T(8,128)(2,1)} copy(bf16[256,256]{1,0:T(8,128)(2,1)} %get-tuple-element.5) | data formatting | bytes 262144
where the time goes:
time: 126 us
  Pallas kernels  122 us (97%)
  local copies, waits for them, and re-layouts  3.1 us (2%)
    pallas_call x1, Pallas kernels, local(): pl.pallas_call(functools.partial(layer_kernel, n, orders, cuts, splits),...  122 us
    unnamed x2, local copies, waits for them, and re-layouts  3.1 us

commit v1 on v0

--- a/solution.py
+++ b/solution.py
@@ -12,6 +12,7 @@
 EXPERTS = 16
 QROWS = 64
 NEG_FILL = -1e30
+LOG2E = 1.4426950408889634
 PIECES = 4
 MESH = pl.DeviceIdType.MESH
 STEPS = KVH // 2
@@ -49,7 +50,7 @@
     down_hbm, wq_hbm, g1_ref, g2_ref,
     stream_ref, nq_ref,
     qb, kb, vb, wo, gate, up, down, wq, accs, mts, acc_ins, mt_ins, parts, part_ins, parts2,
-    part2_ins, rows1, rows2, joined, act, att, load_sems, send_sems, recv_sems,
+    part2_ins, rows1, rows2, joined, act, att, scores, load_sems, send_sems, recv_sems,
 ):
     bits = n.bit_length() - 1
     me = lax.axis_index("seq")
@@ -89,26 +90,27 @@
 
     pairs = H // KVH // 2
     width = pairs * QROWS
-    low = lax.broadcasted_iota(jnp.int32, (span, 2 * HEAD_SIZE), 1) < HEAD_SIZE
-    reach = (
-        me * span
-        + lax.broadcasted_iota(jnp.int32, (span, width), 0)
-        - lax.broadcasted_iota(jnp.int32, (span, width), 1) % QROWS
-    )
+    lanes2 = 2 * HEAD_SIZE
+    k_lane = lax.broadcasted_iota(jnp.int32, (span, lanes2), 1)
+    edge = me * span + lax.broadcasted_iota(jnp.int32, (span, lanes2), 0) - k_lane % QROWS
+    q_lane = lax.broadcasted_iota(jnp.int32, (width, lanes2), 1)
+    q_row = lax.broadcasted_iota(jnp.int32, (width, lanes2), 0)
+    k_low, q_low = k_lane < HEAD_SIZE, q_lane < HEAD_SIZE
+    hit = jnp.where(q_lane % QROWS == q_row % QROWS, 1.0, 0.0).astype(jnp.bfloat16)
+    ones = jnp.ones((16, span), jnp.bfloat16)
+    tile = 128
 
     def attend(g, c):
         at_g = [place(g * slots, order) for order in orders]
+        combos = []
         for r in range(share):
             req = c * share + r
-            allowed = reach <= len_ref[req]
             kv_lanes = pl.ds(pl.multiple_of(g * 128, 128), 128)
             kp = kb[req, :, kv_lanes]
-            vp = vb[req, :, kv_lanes]
+            vt = vb[req, :, kv_lanes].T
             kr = jnp.concatenate([kp[:, HEAD_SIZE:], kp[:, :HEAD_SIZE]], axis=1)
-            zero = jnp.zeros_like(kp)
+            bar = jnp.where(edge > len_ref[req], NEG_FILL, 0.0).astype(jnp.bfloat16)
             for hh in range(2):
-                ke = jnp.where(low, kr if hh else kp, zero)
-                ko = jnp.where(low, zero, kp if hh else kr)
                 first = g * 2 * pairs + hh * pairs
                 qs = jnp.concatenate(
                     [
@@ -120,31 +122,56 @@
                     ],
                     axis=0,
                 ) * jnp.bfloat16(HEAD_SIZE**-0.5)
-                vh = vp[:, hh * HEAD_SIZE : (hh + 1) * HEAD_SIZE]
-                for p, kk in enumerate((ke, ko)):
-                    s = lax.dot_general(
-                        kk, qs, (((1,), (1,)), ((), ())), preferred_element_type=jnp.float32
-                    )
-                    s = jnp.where(allowed, s, NEG_FILL)
-                    m = jnp.max(s, axis=0, keepdims=True)
-                    ch = jnp.exp(s - jnp.maximum(m, NEG_FILL * 0.1))
-                    t = jnp.sum(ch, axis=0, keepdims=True)
-                    acc = lax.dot_general(
-                        vh,
-                        ch.astype(jnp.bfloat16),
-                        (((0,), (0,)), ((), ())),
-                        preferred_element_type=jnp.float32,
-                    ).astype(jnp.bfloat16)
-                    for j in range(pairs):
-                        head = hh * (H // KVH) + 2 * j + p
-                        part, w = divmod(head % per_shard, per_piece)
-                        part = c * splits + part
-                        slot = at_g[part % 2] + place(head // per_shard, orders[part % 2])
-                        src = slice(j * QROWS, (j + 1) * QROWS)
-                        dst = slice(r * QROWS, (r + 1) * QROWS)
-                        accs[part][slot, w * HEAD_SIZE : (w + 1) * HEAD_SIZE, dst] = acc[:, src]
-                        mts[part][slot, w, 0:1, dst] = m[:, src]
-                        mts[part][slot, w, 1:2, dst] = t[:, src]
+                vh = jnp.concatenate([vt[hh * HEAD_SIZE : (hh + 1) * HEAD_SIZE], ones], axis=0)
+                for p in range(2):
+                    kk = kp if hh == p else kr
+                    ka = jnp.where(k_low, bar, kk) if p else jnp.where(k_low, kk, bar)
+                    qa = jnp.where(q_low, hit, qs) if p else jnp.where(q_low, qs, hit)
+                    combos.append((r, hh, p, ka, qa, vh))
+
+        def score(i):
+            ka, qa = combos[i][3:5]
+            top = None
+            for at in range(0, span, tile):
+                s = lax.dot_general(
+                    ka[at : at + tile],
+                    qa,
+                    (((1,), (1,)), ((), ())),
+                    preferred_element_type=jnp.float32,
+                ) * LOG2E
+                scores[i % 2, at : at + tile, :] = s
+                here = jnp.max(s.reshape(tile // 8, 8, width), axis=0)
+                top = here if top is None else jnp.maximum(top, here)
+            return jnp.max(top, axis=0, keepdims=True)
+
+        def weigh(i, m):
+            r, hh, p = combos[i][:3]
+            vh = combos[i][5]
+            base = jnp.maximum(m, NEG_FILL * 0.1)
+            acc = None
+            for at in range(0, span, tile):
+                ch = jnp.exp2((scores[i % 2, at : at + tile, :] - base).astype(jnp.bfloat16))
+                one = jnp.dot(vh[:, at : at + tile], ch, preferred_element_type=jnp.float32)
+                acc = one if acc is None else acc + one
+            t = acc[HEAD_SIZE : HEAD_SIZE + 1]
+            acc = acc[:HEAD_SIZE].astype(jnp.bfloat16)
+            for j in range(pairs):
+                head = hh * (H // KVH) + 2 * j + p
+                part, w = divmod(head % per_shard, per_piece)
+                part = c * splits + part
+                slot = at_g[part % 2] + place(head // per_shard, orders[part % 2])
+                src = slice(j * QROWS, (j + 1) * QROWS)
+                dst = slice(r * QROWS, (r + 1) * QROWS)
+                accs[part][slot, w * HEAD_SIZE : (w + 1) * HEAD_SIZE, dst] = acc[:, src]
+                mts[part][slot, w, 0:1, dst] = m[:, src]
+                mts[part][slot, w, 1:2, dst] = t[:, src]
+
+        last = None
+        for i in range(len(combos) + 1):
+            m = score(i) if i < len(combos) else None
+            if last is not None:
+                weigh(i - 1, last)
+            last = m
 
     def load_wait(*names):
         for name in names:
@@ -213,8 +240,8 @@
                 m1, t1 = mt[mine, w, 0:1, :], mt[mine, w, 1:2, :]
                 m2, t2 = mt_in[other, w, 0:1, :], mt_in[other, w, 1:2, :]
                 m = jnp.maximum(m1, m2)
-                f1 = jnp.exp(m1 - m)
-                f2 = jnp.exp(m2 - m)
+                f1 = jnp.exp2(m1 - m)
+                f2 = jnp.exp2(m2 - m)
                 t = t1 * f1 + t2 * f2
                 rows_w = slice(w * HEAD_SIZE, (w + 1) * HEAD_SIZE)
                 a = (
@@ -475,6 +502,7 @@
             buf(rows, full),
             buf(rows, gate_proj.shape[1]),
             buf(heads, rows),
+            pltpu.VMEM((2, key_cache.shape[1], H // KVH // 2 * QROWS), jnp.float32),
             pltpu.SemaphoreType.DMA((11,)),
             pltpu.SemaphoreType.DMA((phases, bits)),
             pltpu.SemaphoreType.DMA((phases, bits)),

time: 126 us -> 118 us (0.937)
  Pallas kernels: 122 us -> 114 us
    pallas_call x1, Pallas kernels: 122 us -> 114 us  [local(): pl.pallas_call(functools.partial(layer_kernel, n, orders, cuts, splits),...]
where the time goes in v1:
time: 118 us
  Pallas kernels  114 us (97%)
  local copies, waits for them, and re-layouts  3.1 us (3%)
    pallas_call x1, Pallas kernels, local(): pl.pallas_call(functools.partial(layer_kernel, n, orders, cuts, splits),...  114 us
    unnamed x2, local copies, waits for them, and re-layouts  3.1 us

profile of v1, /device:TPU:1, one launch (start us, length us, event | category | flops | bytes accessed | tf_op | source)
XLA Modules:
  0.0 117.6 jit_solution(12670073755467190488)
XLA Ops:
  0.6 113.9 %shard_map.149 = (bf16[16,2880]{1,0:T(8,128)(2,1)}, bf16[256,256]{1,0:T(8,128)(2,1)}) custom-call(s32[4]{0:T(128)} %len_ref.1, bf16[256,4096]{1,0:T(8,128)(2,1)} %q_hbm.1, bf16[4,512,512]{2,1,0:T(8,128)(2,1)} %k_hbm.1, bf16[4,512,512]{2,1,0:T(8,128)(2,1)} %v_hbm.1, bf16[16,2880]{1,0:T(8,128)(2,1)} %resid_ref.1, s32[4,16]{1,0:T(4,128)} %bitcast.8, ...), custom_call_target="tpu_custom_call" | custom-call | tf_op jit(solution)/shard_map/pallas_call | solution.py:475
  114.5 1.5 %copy.18 = bf16[16,2880]{1,0:T(8,128)(2,1)} copy(bf16[16,2880]{1,0:T(8,128)(2,1)} %get-tuple-element.4) | data formatting | bytes 184320
  116.0 1.6 %copy.19 = bf16[256,256]{1,0:T(8,128)(2,1)} copy(bf16[256,256]{1,0:T(8,128)(2,1)} %get-tuple-element.5) | data formatting | bytes 262144

commit v2 on v1

--- a/solution.py
+++ b/solution.py
@@ -13,7 +13,7 @@
 QROWS = 64
 NEG_FILL = -1e30
 LOG2E = 1.4426950408889634
-PIECES = 4
+PIECES = 6
 MESH = pl.DeviceIdType.MESH
 STEPS = KVH // 2
 
@@ -342,7 +342,10 @@
 
         chunks(parts[c].shape[2], 256, project)
         exchange[c].start(0)
-    for j in range(bits):
+        if c:
+            exchange[c - 1].finish(0)
+    exchange[pieces - 1].finish(0)
+    for j in range(1, bits):
         for c in range(pieces):
             exchange[c].finish(j)
     hidden = (
@@ -412,7 +415,10 @@
 
         chunks(parts2[c].shape[2], 256, outer)
         exchange[c].start(0)
-    for j in range(bits):
+        if c:
+            exchange[c - 1].finish(0)
+    exchange[pieces - 1].finish(0)
+    for j in range(1, bits):
         for c in range(pieces):
             exchange[c].finish(j)
     stream = (
@@ -430,6 +436,11 @@
     ).astype(jnp.bfloat16)
     for copy in sends:
         copy.wait_send()
+
+
+def hand_over(stream_in, nq_in, stream_ref, nq_ref):
+    stream_ref[...] = stream_in[...]
+    nq_ref[...] = nq_in[...]
 
 
 def local(
@@ -472,7 +483,7 @@
     acc = lambda: tuple(buf(n, heads // splits, rows // 2) for _ in range(2 * splits))
     mt_shape = (n, per_shard // splits, 2, rows // 2)
     mt = lambda: tuple(pltpu.VMEM(mt_shape, jnp.float32) for _ in range(2 * splits))
-    return pl.pallas_call(
+    stream, nq = pl.pallas_call(
         functools.partial(layer_kernel, n, orders, cuts, splits),
         out_shape=(
             jax.ShapeDtypeStruct((tok, d), bf),
@@ -514,6 +525,15 @@
         lengths, queries, key_cache, value_cache, resid_in, expert_ids.T, expert_weights.T,
         out_proj.T, gate_proj.T, up_proj.T, down_proj, query_proj, moe_gain, attn_gain,
     )
+    return pl.pallas_call(
+        hand_over,
+        out_shape=(
+            jax.ShapeDtypeStruct(stream.shape, bf),
+            jax.ShapeDtypeStruct(nq.shape, bf),
+        ),
+        in_specs=[vmem, vmem],
+        out_specs=(vmem, vmem),
+    )(stream, nq)
 
 
 def solution(mesh):

time: 118 us -> 112 us (0.949)
  local copies, waits for them, and re-layouts: 3.1 us -> 0 us
  Pallas kernels: 114 us -> 111 us
    pallas_call x1, Pallas kernels: 114 us -> 110 us  [local(): pl.pallas_call(functools.partial(layer_kernel, n, orders, cuts, splits),...]
    unnamed x2 -> x0, local copies, waits for them, and re-layouts: 3.1 us -> none
    pallas_call x0 -> x1, Pallas kernels: none -> 1.64 us  [local(): pl.pallas_call(hand_over, out_shape=(jax.ShapeDtypeStruct(stream.shape, b...]
where the time goes in v2:
time: 112 us
  Pallas kernels  111 us (99%)
    pallas_call x1, Pallas kernels, local(): pl.pallas_call(functools.partial(layer_kernel, n, orders, cuts, splits),...  110 us

profile of v2, /device:TPU:1, one launch (start us, length us, event | category | flops | bytes accessed | tf_op | source)
XLA Modules:
  0.0 111.8 jit_solution(10292552857127864424)
XLA Ops:
  0.6 109.5 %shard_map.149 = (bf16[16,2880]{1,0:T(8,128)(2,1)}, bf16[256,256]{1,0:T(8,128)(2,1)}) custom-call(s32[4]{0:T(128)} %len_ref.1, bf16[256,4096]{1,0:T(8,128)(2,1)} %q_hbm.1, bf16[4,512,512]{2,1,0:T(8,128)(2,1)} %k_hbm.1, bf16[4,512,512]{2,1,0:T(8,128)(2,1)} %v_hbm.1, bf16[16,2880]{1,0:T(8,128)(2,1)} %resid_ref.1, s32[4,16]{1,0:T(4,128)} %bitcast.8, ...), custom_call_target="tpu_custom_call" | custom-call | tf_op jit(solution)/shard_map/pallas_call | solution.py:486
  110.2 1.6 %shard_map.150 = (bf16[16,2880]{1,0:T(8,128)(2,1)}, bf16[256,256]{1,0:T(8,128)(2,1)}) custom-call(bf16[16,2880]{1,0:T(8,128)(2,1)} %get-tuple-element.4.stream_in, bf16[256,256]{1,0:T(8,128)(2,1)} %get-tuple-element.5.nq_in), custom_call_target="tpu_custom_call" | custom-call | tf_op jit(solution)/shard_map/pallas_call | solution.py:528

commit v3 on v2

--- a/solution.py
+++ b/solution.py
@@ -274,6 +274,12 @@
 
         return [Halving(c, [bufs[c]], [inboxes[c]], [phase + c], adder(c)) for c in range(pieces)], sums
 
+    def join(bufs, c):
+        for i in range(n):
+            joined[i * tok : (i + 1) * tok, cuts[c] : cuts[c] + bufs[c].shape[2]] = bufs[c][
+                place(i, orders[c % 2])
+            ]
+
     def gather(bufs, phase):
         bases = [place(me, orders[c % 2]) for c in range(pieces)]
 
@@ -288,13 +294,8 @@
                 flying[c].wait_recv()
                 if j:
                     flying[c] = start(c, j - 1)
-
-    def join(bufs):
-        for i in range(n):
-            for c in range(pieces):
-                joined[i * tok : (i + 1) * tok, cuts[c] : cuts[c] + bufs[c].shape[2]] = bufs[c][
-                    place(i, orders[c % 2])
-                ]
+                else:
+                    join(bufs, c)
 
     def spread(bufs, c, start, size, val):
         for i in range(n):
@@ -340,7 +341,7 @@
             ).astype(jnp.bfloat16)
             spread(parts, c, start, size, val)
 
-        chunks(parts[c].shape[2], 256, project)
+        chunks(parts[c].shape[2], 512, project)
         exchange[c].start(0)
         if c:
             exchange[c - 1].finish(0)
@@ -371,7 +372,6 @@
     gather(rows1, 4 * splits + pieces)
 
     load_wait("gate", "up", "down")
-    join(rows1)
     normed = joined[:, :d]
     tags = joined[:, d:].astype(jnp.float32)
     expert = me // (n // EXPERTS)
@@ -413,7 +413,7 @@
             ).astype(jnp.bfloat16)
             spread(parts2, c, start, size, val)
 
-        chunks(parts2[c].shape[2], 256, outer)
+        chunks(parts2[c].shape[2], 512, outer)
         exchange[c].start(0)
         if c:
             exchange[c - 1].finish(0)
@@ -430,7 +430,6 @@
         rows2[c][here[c]] = normed_next[:, cuts[c] : ends[c]]
     gather(rows2, 4 * splits + 3 * pieces)
     load_wait("wq")
-    join(rows2)
     nq_ref[...] = jnp.dot(
         joined[:, :d], wq[...], preferred_element_type=jnp.float32
     ).astype(jnp.bfloat16)

time: 112 us -> 111 us (level)
    pallas_call x1, Pallas kernels: 110 us -> 108 us  [local(): pl.pallas_call(functools.partial(layer_kernel, n, orders, cuts, splits),...]
where the time goes in v3:
time: 111 us
  Pallas kernels  110 us (99%)
    pallas_call x1, Pallas kernels, local(): pl.pallas_call(functools.partial(layer_kernel, n, orders, cuts, splits),...  108 us

profile of v3, /device:TPU:1, one launch (start us, length us, event | category | flops | bytes accessed | tf_op | source)
XLA Modules:
  0.0 110.7 jit_solution(1743580737965321203)
XLA Ops:
  0.6 108.4 %shard_map.149 = (bf16[16,2880]{1,0:T(8,128)(2,1)}, bf16[256,256]{1,0:T(8,128)(2,1)}) custom-call(s32[4]{0:T(128)} %len_ref.1, bf16[256,4096]{1,0:T(8,128)(2,1)} %q_hbm.1, bf16[4,512,512]{2,1,0:T(8,128)(2,1)} %k_hbm.1, bf16[4,512,512]{2,1,0:T(8,128)(2,1)} %v_hbm.1, bf16[16,2880]{1,0:T(8,128)(2,1)} %resid_ref.1, s32[4,16]{1,0:T(4,128)} %bitcast.8, ...), custom_call_target="tpu_custom_call" | custom-call | tf_op jit(solution)/shard_map/pallas_call | solution.py:485
  109.0 1.6 %shard_map.150 = (bf16[16,2880]{1,0:T(8,128)(2,1)}, bf16[256,256]{1,0:T(8,128)(2,1)}) custom-call(bf16[16,2880]{1,0:T(8,128)(2,1)} %get-tuple-element.4.stream_in, bf16[256,256]{1,0:T(8,128)(2,1)} %get-tuple-element.5.nq_in), custom_call_target="tpu_custom_call" | custom-call | tf_op jit(solution)/shard_map/pallas_call | solution.py:527
